TPU v7x, 32 devices: a whole 2x2x4 slice. The times are simulated.
32 devices in a mesh: beams: 2 (over x), trials: 16 (over z, y, core).
Axes of the slice: x: 2, y: 2, z: 4, core: 2. Of those that a mesh axis runs over, the one named last changes fastest.
Arguments:
- spectra: bfloat16 [4096, 8192], P(('beams', 'trials')), parts along dimension 0, may hold values from -12 to 12
- delays: int32 [64, 16], P('trials'), may hold values from 0 to 56
- spans: int32 [16], replicated, may hold values from 1 to 8, as said below
- widths: int32 [8], replicated, may hold values from 1 to 128
Outputs:
- boxcar_out: float32 [128, 8, 1024], P(('beams', 'trials')), parts along dimension 0
There are 2 independent parts, one for each index of `beams`. A program takes and returns all parts, laid end to end along the dimension named above; an argument that names none is the same for every part. Nothing has to cross between parts.
Inputs may be any that keep to these rules, and one draw needn't show every extreme that they name: Ranges come in pairs: spans[2 i] + spans[2 i + 1] = 9 for every i; some range has exactly 8 live blocks.
All inputs are finite; a program needn't handle non-finite values.
Results may differ from a plain program's by a relative error of at most 0.0003.
Values sent between devices are 32-bit elements; how exact they have to be, the bound alone decides.
No kernel may reach another device: no remote copies, remote signals or barrier semaphores. Data moves between devices by JAX's collectives and lax.ppermute only.
A program may use at most 64 MiB of HBM per device.

v0:
```python
import jax
import jax.numpy as jnp
from jax import lax
from jax.sharding import PartitionSpec as P

CH_SUB = 128
SAMPLE_COUNT = 8192
SUBT = 2
SHIFT = 8
SPAN = 8
KMAX = 8
NB = 64
OUT = 1024


def boxcars(trial, widths):
    total_len = trial.shape[1]
    prefix = jnp.cumsum(trial, axis=1)
    padded_series = jnp.concatenate([jnp.zeros_like(prefix), prefix], axis=1)

    def one_width(width):
        start = total_len - width
        lagged = lax.dynamic_slice_in_dim(padded_series, start, total_len, 1)
        return (prefix - lagged) / jnp.sqrt(width.astype(jnp.float32))

    return jax.vmap(one_width, out_axes=1)(widths)


def finish(trial, live, widths):
    trial = jnp.where(jnp.arange(trial.shape[1])[None, :] < live, trial, jnp.float32(0.0))
    return boxcars(trial, widths)


def subband_series(spectra, channel_mean, channels):
    chan = jnp.arange(CH_SUB)
    level = jnp.arange(SUBT)
    delay_in = level[:, None] * SHIFT * chan[None, :] // CH_SUB
    select = (delay_in[:, None, :] == jnp.arange(KMAX)[None, :, None]).reshape(SUBT * KMAX, CH_SUB)
    counts = jnp.sum(select.astype(jnp.float32), axis=1)
    grouped = jnp.dot(select.astype(jnp.bfloat16), spectra, preferred_element_type=jnp.float32)
    grouped = grouped - counts[:, None] * channel_mean[None, :]
    grouped = jnp.pad(grouped.reshape(SUBT, KMAX, SAMPLE_COUNT), ((0, 0), (0, 0), (0, KMAX)))
    time_series = grouped[:, 0, 0:SAMPLE_COUNT]
    for lag in range(1, KMAX):
        time_series = time_series + grouped[:, lag, lag : lag + SAMPLE_COUNT]
    return time_series / jnp.sqrt(jnp.float32(channels))


def on_device(spectra, delays, spans, widths):
    group = lax.axis_size("trials")
    mine = lax.axis_index("trials")
    channels = CH_SUB * group
    ones_row = jnp.ones((1, CH_SUB), jnp.bfloat16)
    local_sums = jnp.dot(ones_row, spectra, preferred_element_type=jnp.float32)[0]
    channel_mean = lax.psum(local_sums, "trials") / channels
    time_series = subband_series(spectra, channel_mean, channels)
    offsets = jnp.arange(SPAN)
    live = lax.dynamic_index_in_dim(spans, mine, 0, keepdims=False) * 128
    tr_dev = delays.shape[0]
    own_delays = lax.all_to_all(delays, "trials", split_axis=1, concat_axis=0, tiled=True)[:, 0]
    series_blocks = time_series.reshape(SUBT, NB, 128)
    trial_sub = jnp.arange(tr_dev * group) % SUBT
    window = series_blocks[trial_sub[:, None], own_delays[:, None] + offsets[None, :]]
    window = window.reshape(group, tr_dev, OUT)
    return finish(
        jnp.sum(lax.all_to_all(window, "trials", split_axis=0, concat_axis=0, tiled=True), axis=0),
        live,
        widths,
    )


def solution(mesh):
    in_specs = (P(("beams", "trials"), None), P("trials", None), P(), P())
    out_specs = P(("beams", "trials"), None, None)
    return jax.shard_map(
        on_device, mesh=mesh, in_specs=in_specs, out_specs=out_specs, check_vma=False
    )
```

profile of v0, /device:TPU:0, one launch (start us, length us, event | category | flops | bytes accessed | tf_op | source)
XLA Modules:
  0.0 105.8 jit_solution(5896541626378385895)
XLA Ops:
  0.0 1.5 %copy.11 = s32[4,16,1]{0,2,1:T(1,128)} copy(s32[4,16,1]{1,0,2:T(4,128)} %bitcast.41) | data formatting | bytes 512 | tf_op jit(solution)/shard_map/all_to_all | solution.py:60
  1.5 7.4 %all-to-all-start = ((s32[4,16,1]{0,2,1:T(1,128)}), s32[4,16,1]{0,2,1:T(1,128)S(1)}, u32[]{:S(2)}, u32[]{:S(2)}) async-start(s32[4,16,1]{0,2,1:T(1,128)} %copy.11), calls=%async_computation | async-start | bytes 16384 | tf_op jit(solution)/shard_map/all_to_all | solution.py:60
  9.3 61.9 %psum.7 = f32[8192]{0:T(1024)S(1)} all-reduce(f32[8192]{0:T(1024)S(1)} %bitcast.38), channel_id=1, replica_groups=mesh['beams'=2,'trials'=16] {'trials'}, use_global_device_ids=true, to_apply=%region_1.2 | all-reduce | flops 8192 | bytes 65536 | tf_op jit(solution)/shard_map/psum | solution.py:55
  72.0 1.0 fusion.8
  73.4 3.7 %gather_fusion = f32[512,128]{1,0:T(8,128)S(1)} fusion(f32[2,64,128]{2,1,0:T(8,128)S(1)} %bitcast.35, s32[512]{0:T(512)S(1)} %reshape.197), kind=kCustom, calls=%fused_computation | custom fusion | bytes 528384 | tf_op jit(solution)/shard_map/gather | solution.py:63
  77.0 0.8 reshape.171
  77.8 3.5 %all-to-all-start.1 = ((f32[16,4,1024]{2,1,0:T(4,128)}), f32[16,4,1024]{2,1,0:T(4,128)S(1)}, u32[]{:S(2)}, u32[]{:S(2)}) async-start(f32[16,4,1024]{2,1,0:T(4,128)} %reshape.171), calls=%async_computation.1 | async-start | bytes 524288 | tf_op jit(solution)/shard_map/all_to_all | solution.py:66
  81.4 0.6 dynamic_slice.4
  82.7 8.7 %all-to-all-done.1 = f32[16,4,1024]{2,1,0:T(4,128)S(1)} async-done(((f32[16,4,1024]{2,1,0:T(4,128)}), f32[16,4,1024]{2,1,0:T(4,128)S(1)}, u32[]{:S(2)}, u32[]{:S(2)}) %all-to-all-start.1) | async-done | bytes 262176 | tf_op jit(solution)/shard_map/all_to_all | solution.py:66
  91.4 1.1 %reduce-window.6 = f32[4,8,128]{2,1,0:T(8,128)S(1)} reduce-window(f32[4,8,128]{2,1,0:T(8,128)S(1)} %bitcast_select_fusion, f32[]{:T(128)} %constant.65.clone.1), window={size=1x1x128 pad=0_0x0_0x127_0}, to_apply=%region_3.4 | reduce-window | flops 520192 | bytes 32772 | tf_op jit(solution)/shard_map/reduce-window
  93.0 12.1 %while.1 = (s32[]{:T(128)}, f32[4,2048]{1,0:T(4,128)S(1)}, s32[8,2]{0,1:T(2,128)S(1)}, f32[8,4,1024]{2,0,1:T(8,128)S(1)}, s32[]{:T(128)}, /*index=5*/s32[]{:T(128)}) while((s32[]{:T(128)}, f32[4,2048]{1,0:T(4,128)S(1)}, s32[8,2]{0,1:T(2,128)S(1)}, f32[8,4,1024]{2,0,1:T(8,128)S(1)}, s32[]{:T(128)}, /*index=5*/s32[]{:T(128)}) %tuple.16), condition=%wide.while_cond, body=%wide.while_body.sunk | while | flops 2 | bytes 98417 | solution.py:23
  93.1 0.5 slice.108
  93.6 0.7 dynamic-slice_bitcast_fusion.2
  94.6 0.5 slice.108
  95.1 0.7 dynamic-slice_bitcast_fusion.2
  96.1 0.5 slice.108
  96.6 0.7 dynamic-slice_bitcast_fusion.2
  98.1 0.7 dynamic-slice_bitcast_fusion.2
  99.1 0.5 slice.108
  99.6 0.7 dynamic-slice_bitcast_fusion.2
  101.1 0.7 dynamic-slice_bitcast_fusion.2
  102.6 0.7 dynamic-slice_bitcast_fusion.2
  104.2 0.7 dynamic-slice_bitcast_fusion.2
  105.1 0.7 divide_bitcast_fusion
  (61 shorter events, 6.0 us)
Async XLA Ops:
  0.0 8.9 %copy-start = (bf16[128,8192]{1,0:T(8,128)(2,1)S(1)}, bf16[128,8192]{1,0:T(8,128)(2,1)}, u32[]{:S(2)}) copy-start(bf16[128,8192]{1,0:T(8,128)(2,1)} %param.4) | copy-start | bytes 6291460
  1.5 71.5 %all-to-all-start = ((s32[4,16,1]{0,2,1:T(1,128)}), s32[4,16,1]{0,2,1:T(1,128)S(1)}, u32[]{:S(2)}, u32[]{:S(2)}) async-start(s32[4,16,1]{0,2,1:T(1,128)} %copy.11), calls=%async_computation | async-start | bytes 16384 | tf_op jit(solution)/shard_map/all_to_all | solution.py:60
  72.0 9.3 %copy-start.2 = (s32[8]{0:T(128)S(1)}, s32[8]{0:T(128)}, u32[]{:S(2)}) copy-start(s32[8]{0:T(128)} %param.7) | copy-start | bytes 100
  72.0 9.4 %copy-start.1 = (s32[16]{0:T(128)S(1)}, s32[16]{0:T(128)}, u32[]{:S(2)}) copy-start(s32[16]{0:T(128)} %param.6) | copy-start | bytes 196
  77.8 13.5 %all-to-all-start.1 = ((f32[16,4,1024]{2,1,0:T(4,128)}), f32[16,4,1024]{2,1,0:T(4,128)S(1)}, u32[]{:S(2)}, u32[]{:S(2)}) async-start(f32[16,4,1024]{2,1,0:T(4,128)} %reshape.171), calls=%async_computation.1 | async-start | bytes 524288 | tf_op jit(solution)/shard_map/all_to_all | solution.py:66
where the time goes:
time: 106 us
  blocking collectives  61.9 us (58%)
  local copies, waits for them, and re-layouts  18.9 us (18%)
  starting transfers between devices  10.9 us (10%)
  waiting for transfers between devices  8.69 us (8%)
  other arithmetic  3.51 us (3%)
    psum x1, blocking collectives, on_device(): channel_mean = lax.psum(local_sums, 'trials') / channels  61.9 us
    gather x40, local copies, waits for them, and re-layouts  11.8 us
    all_to_all x1, waiting for transfers between devices, on_device(): lax.all_to_all(window, 'trials', split_axis=0, concat_axis=0, tiled=True)  8.69 us
    all_to_all x1, starting transfers between devices, on_device(): lax.all_to_all(delays, 'trials', split_axis=1, concat_axis=0, tiled=True)  7.39 us
    gather x1, local copies, waits for them, and re-layouts, on_device(): series_blocks[trial_sub[:, None], own_delays[:, None] + offsets[None, :]]  3.66 us
    all_to_all x1, starting transfers between devices, on_device(): lax.all_to_all(window, 'trials', split_axis=0, concat_axis=0, tiled=True)  3.53 us
  transfers between devices with their start and end apart: 2, of which 1 were waited for; matrix products, arithmetic and copies ran while one was open for 3% of the time, Pallas kernels for 0%

commit v1 on v0

--- a/solution.py
+++ b/solution.py
@@ -52,7 +52,7 @@
     channels = CH_SUB * group
     ones_row = jnp.ones((1, CH_SUB), jnp.bfloat16)
     local_sums = jnp.dot(ones_row, spectra, preferred_element_type=jnp.float32)[0]
-    channel_mean = lax.psum(local_sums, "trials") / channels
+    channel_mean = jnp.sum(lax.all_gather(local_sums, "trials"), axis=0) / channels
     time_series = subband_series(spectra, channel_mean, channels)
     offsets = jnp.arange(SPAN)
     live = lax.dynamic_index_in_dim(spans, mine, 0, keepdims=False) * 128

time: 106 us -> 67.7 us (0.64)
  blocking collectives: 61.9 us -> 23.2 us
    psum x1 -> x0, blocking collectives: 61.9 us -> none  [on_device(): channel_mean = lax.psum(local_sums, 'trials') / channels]
    all_gather x0 -> x1, blocking collectives: none -> 23.2 us  [on_device(): lax.all_gather(local_sums, 'trials')]
  transfers between devices with their start and end apart: 2 -> 2, of which waited for: 1 -> 1; matrix products, arithmetic and copies ran while one was open for 3% -> 4% of each run, Pallas kernels for 0% -> 0%
where the time goes in v1:
time: 67.7 us; the launch traced here: 67.4 us
  blocking collectives  23.2 us (34%)
  local copies, waits for them, and re-layouts  19 us (28%)
  starting transfers between devices  10.9 us (16%)
  waiting for transfers between devices  8.69 us (13%)
  other arithmetic  3.59 us (5%)
  between operations  0.84 us (1%)
  matrix products  0.82 us (1%)
    all_gather x1, blocking collectives, on_device(): lax.all_gather(local_sums, 'trials')  23.2 us
    gather x40, local copies, waits for them, and re-layouts  11.8 us
    all_to_all x1, waiting for transfers between devices, on_device(): lax.all_to_all(window, 'trials', split_axis=0, concat_axis=0, tiled=True)  8.69 us
    all_to_all x1, starting transfers between devices, on_device(): lax.all_to_all(delays, 'trials', split_axis=1, concat_axis=0, tiled=True)  7.39 us
    gather x1, local copies, waits for them, and re-layouts, on_device(): series_blocks[trial_sub[:, None], own_delays[:, None] + offsets[None, :]]  3.66 us
    all_to_all x1, starting transfers between devices, on_device(): lax.all_to_all(window, 'trials', split_axis=0, concat_axis=0, tiled=True)  3.53 us
    all_to_all x2, local copies, waits for them, and re-layouts, on_device(): lax.all_to_all(delays, 'trials', split_axis=1, concat_axis=0, tiled=True)  1.53 us
  transfers between devices with their start and end apart: 2, of which 1 were waited for; matrix products, arithmetic and copies ran while one was open for 4% of the time, Pallas kernels for 0%

profile of v1, /device:TPU:0, one launch (start us, length us, event | category | flops | bytes accessed | tf_op | source)
XLA Modules:
  0.0 67.4 jit_solution(1295108298589113835)
XLA Ops:
  0.0 1.5 %copy.11 = s32[4,16,1]{0,2,1:T(1,128)} copy(s32[4,16,1]{1,0,2:T(4,128)} %bitcast.41) | data formatting | bytes 512 | tf_op jit(solution)/shard_map/all_to_all | solution.py:60
  1.5 7.4 %all-to-all-start = ((s32[4,16,1]{0,2,1:T(1,128)}), s32[4,16,1]{0,2,1:T(1,128)S(1)}, u32[]{:S(2)}, u32[]{:S(2)}) async-start(s32[4,16,1]{0,2,1:T(1,128)} %copy.11), calls=%async_computation | async-start | bytes 16384 | tf_op jit(solution)/shard_map/all_to_all | solution.py:60
  9.3 23.2 %all-gather = f32[131072]{0:T(1024)S(1)} all-gather(f32[8192]{0:T(1024)S(1)} %bitcast.38), channel_id=2, replica_groups=mesh['beams'=2,'trials'=16] {'trials'}, dimensions={0}, use_global_device_ids=true | all-gather | bytes 557056 | tf_op jit(solution)/shard_map/all_gather | solution.py:55
  33.6 1.0 %fusion.8 = f32[2,1,8192]{2,1,0:T(1,128)S(1)} fusion(f32[2,8,8192]{2,1,0:T(8,128)S(1)} %fusion), kind=kLoop, calls=%fused_computation.21 | loop fusion | flops 131072 | bytes 655360 | tf_op jit(solution)/shard_map/div | solution.py:46
  34.9 3.7 %gather_fusion = f32[512,128]{1,0:T(8,128)S(1)} fusion(f32[2,64,128]{2,1,0:T(8,128)S(1)} %bitcast.35, s32[512]{0:T(512)S(1)} %reshape.198), kind=kCustom, calls=%fused_computation | custom fusion | bytes 528384 | tf_op jit(solution)/shard_map/gather | solution.py:63
  38.6 0.8 %reshape.172 = f32[16,4,1024]{2,1,0:T(4,128)} reshape(f32[512,128]{1,0:T(8,128)S(1)} %gather_fusion) | data formatting | bytes 524288 | tf_op jit(solution)/shard_map/reshape | solution.py:64
  39.3 3.5 %all-to-all-start.1 = ((f32[16,4,1024]{2,1,0:T(4,128)}), f32[16,4,1024]{2,1,0:T(4,128)S(1)}, u32[]{:S(2)}, u32[]{:S(2)}) async-start(f32[16,4,1024]{2,1,0:T(4,128)} %reshape.172), calls=%async_computation.1 | async-start | bytes 524288 | tf_op jit(solution)/shard_map/all_to_all | solution.py:66
  42.9 0.6 dynamic_slice.4
  44.2 8.7 %all-to-all-done.1 = f32[16,4,1024]{2,1,0:T(4,128)S(1)} async-done(((f32[16,4,1024]{2,1,0:T(4,128)}), f32[16,4,1024]{2,1,0:T(4,128)S(1)}, u32[]{:S(2)}, u32[]{:S(2)}) %all-to-all-start.1) | async-done | bytes 262176 | tf_op jit(solution)/shard_map/all_to_all | solution.py:66
  53.0 1.1 %reduce-window.6 = f32[4,8,128]{2,1,0:T(8,128)S(1)} reduce-window(f32[4,8,128]{2,1,0:T(8,128)S(1)} %bitcast_select_fusion, f32[]{:T(128)} %constant.65.clone.1), window={size=1x1x128 pad=0_0x0_0x127_0}, to_apply=%region_3.4 | reduce-window | flops 520192 | bytes 32772 | tf_op jit(solution)/shard_map/reduce-window
  54.5 12.1 %while.1 = (s32[]{:T(128)}, f32[4,2048]{1,0:T(4,128)S(1)}, s32[8,2]{0,1:T(2,128)S(1)}, f32[8,4,1024]{2,0,1:T(8,128)S(1)}, s32[]{:T(128)}, /*index=5*/s32[]{:T(128)}) while((s32[]{:T(128)}, f32[4,2048]{1,0:T(4,128)S(1)}, s32[8,2]{0,1:T(2,128)S(1)}, f32[8,4,1024]{2,0,1:T(8,128)S(1)}, s32[]{:T(128)}, /*index=5*/s32[]{:T(128)}) %tuple.16), condition=%wide.while_cond, body=%wide.while_body.sunk | while | flops 2 | bytes 98417 | solution.py:23
  54.6 0.5 slice.108
  55.1 0.7 %dynamic-slice_bitcast_fusion.2 = f32[1,4,1024]{2,1,0:T(4,128)S(1)} fusion(f32[4,2048]{1,0:T(4,128)S(1)} %get-tuple-element.59, s32[]{:T(128)} %bitcast.34), kind=kLoop, calls=%fused_computation.1.clone.1 | loop fusion | bytes 32772 | tf_op jit(solution)/shard_map/vmap()/gather
  56.1 0.5 slice.108
  56.7 0.7 %dynamic-slice_bitcast_fusion.2 = f32[1,4,1024]{2,1,0:T(4,128)S(1)} fusion(f32[4,2048]{1,0:T(4,128)S(1)} %get-tuple-element.59, s32[]{:T(128)} %bitcast.34), kind=kLoop, calls=%fused_computation.1.clone.1 | loop fusion | bytes 32772 | tf_op jit(solution)/shard_map/vmap()/gather
  57.6 0.5 slice.108
  58.2 0.7 %dynamic-slice_bitcast_fusion.2 = f32[1,4,1024]{2,1,0:T(4,128)S(1)} fusion(f32[4,2048]{1,0:T(4,128)S(1)} %get-tuple-element.59, s32[]{:T(128)} %bitcast.34), kind=kLoop, calls=%fused_computation.1.clone.1 | loop fusion | bytes 32772 | tf_op jit(solution)/shard_map/vmap()/gather
  59.7 0.7 %dynamic-slice_bitcast_fusion.2 = f32[1,4,1024]{2,1,0:T(4,128)S(1)} fusion(f32[4,2048]{1,0:T(4,128)S(1)} %get-tuple-element.59, s32[]{:T(128)} %bitcast.34), kind=kLoop, calls=%fused_computation.1.clone.1 | loop fusion | bytes 32772 | tf_op jit(solution)/shard_map/vmap()/gather
  60.7 0.5 slice.108
  61.2 0.7 %dynamic-slice_bitcast_fusion.2 = f32[1,4,1024]{2,1,0:T(4,128)S(1)} fusion(f32[4,2048]{1,0:T(4,128)S(1)} %get-tuple-element.59, s32[]{:T(128)} %bitcast.34), kind=kLoop, calls=%fused_computation.1.clone.1 | loop fusion | bytes 32772 | tf_op jit(solution)/shard_map/vmap()/gather
  62.7 0.7 %dynamic-slice_bitcast_fusion.2 = f32[1,4,1024]{2,1,0:T(4,128)S(1)} fusion(f32[4,2048]{1,0:T(4,128)S(1)} %get-tuple-element.59, s32[]{:T(128)} %bitcast.34), kind=kLoop, calls=%fused_computation.1.clone.1 | loop fusion | bytes 32772 | tf_op jit(solution)/shard_map/vmap()/gather
  64.2 0.7 %dynamic-slice_bitcast_fusion.2 = f32[1,4,1024]{2,1,0:T(4,128)S(1)} fusion(f32[4,2048]{1,0:T(4,128)S(1)} %get-tuple-element.59, s32[]{:T(128)} %bitcast.34), kind=kLoop, calls=%fused_computation.1.clone.1 | loop fusion | bytes 32772 | tf_op jit(solution)/shard_map/vmap()/gather
  65.7 0.7 %dynamic-slice_bitcast_fusion.2 = f32[1,4,1024]{2,1,0:T(4,128)S(1)} fusion(f32[4,2048]{1,0:T(4,128)S(1)} %get-tuple-element.59, s32[]{:T(128)} %bitcast.34), kind=kLoop, calls=%fused_computation.1.clone.1 | loop fusion | bytes 32772 | tf_op jit(solution)/shard_map/vmap()/gather
  66.6 0.7 %divide_bitcast_fusion = f32[4,8,1024]{2,1,0:T(8,128)} fusion(f32[8,4,1024]{2,0,1:T(8,128)S(1)} %get-tuple-element.12, f32[8]{0:T(128)S(1)} %convert_sqrt_fusion, f32[4,1024]{1,0:T(4,128)S(1)} %bitcast.37), kind=kLoop, calls=%fused_computation.12 | loop fusion | flops 65536 | bytes 278560 | tf_op jit(solution)/shard_map/vmap()/div | solution.py:24
  (63 shorter events, 6.1 us)
Async XLA Ops:
  0.0 8.9 %copy-start = (bf16[128,8192]{1,0:T(8,128)(2,1)S(1)}, bf16[128,8192]{1,0:T(8,128)(2,1)}, u32[]{:S(2)}) copy-start(bf16[128,8192]{1,0:T(8,128)(2,1)} %param.4) | copy-start | bytes 6291460
  1.5 33.1 %all-to-all-start = ((s32[4,16,1]{0,2,1:T(1,128)}), s32[4,16,1]{0,2,1:T(1,128)S(1)}, u32[]{:S(2)}, u32[]{:S(2)}) async-start(s32[4,16,1]{0,2,1:T(1,128)} %copy.11), calls=%async_computation | async-start | bytes 16384 | tf_op jit(solution)/shard_map/all_to_all | solution.py:60
  33.5 9.3 %copy-start.2 = (s32[8]{0:T(128)S(1)}, s32[8]{0:T(128)}, u32[]{:S(2)}) copy-start(s32[8]{0:T(128)} %param.7) | copy-start | bytes 100
  33.5 9.4 %copy-start.1 = (s32[16]{0:T(128)S(1)}, s32[16]{0:T(128)}, u32[]{:S(2)}) copy-start(s32[16]{0:T(128)} %param.6) | copy-start | bytes 196
  39.3 13.5 %all-to-all-start.1 = ((f32[16,4,1024]{2,1,0:T(4,128)}), f32[16,4,1024]{2,1,0:T(4,128)S(1)}, u32[]{:S(2)}, u32[]{:S(2)}) async-start(f32[16,4,1024]{2,1,0:T(4,128)} %reshape.172), calls=%async_computation.1 | async-start | bytes 524288 | tf_op jit(solution)/shard_map/all_to_all | solution.py:66
